TPU v7x, 32 devices: a whole 2x2x4 slice. The times are simulated.
32 devices in a mesh: grp: 2 (over x), ctx: 16 (over z, y, core).
Axes of the slice: x: 2, y: 2, z: 4, core: 2. Of those that a mesh axis runs over, the one named last changes fastest.
Arguments:
- queries: bfloat16 [960, 4096], P(None, ('grp', 'ctx')), parts along dimension 1, may hold values from -6 to 6
- key_rows: bfloat16 [960, 4096], P(None, ('grp', 'ctx')), parts along dimension 1, may hold values from -6 to 6
- value_rows: bfloat16 [960, 4096], P(None, ('grp', 'ctx')), parts along dimension 1, may hold values from -6 to 6
- short_taps: float32 [3, 960, 7], replicated, may hold values from -2 to 2
- long_filter: bfloat16 [960, 2048], P('ctx'), may hold values from -0.125 to 0.125
Outputs:
- mixed: bfloat16 [960, 4096], P(None, ('grp', 'ctx')), parts along dimension 1
There are 2 independent parts, one for each index of `grp`. A program takes and returns all parts, laid end to end along the dimension named above; an argument that names none is the same for every part. Nothing has to cross between parts.
All inputs are finite; a program needn't handle non-finite values.
Results may differ from a plain program's by a relative error of at most 0.0057.
Values may be sent and summed in bfloat16 or wider, within the bound.
A program may use at most 64 MiB of HBM per device.

v0:
```python
import math

import jax
import jax.numpy as jnp
from jax import lax
from jax.sharding import PartitionSpec as P

TAPS = 7


precise = lax.Precision.HIGH


def with_halo(value, sides, width):
    for axis, dim in sides:
        size, length = (lax.axis_size(axis), value.shape[dim])
        up = [(i, (i + 1) % size) for i in range(size - 1)]
        down = [(j, i) for i, j in up]
        last = lax.slice_in_dim(value, length - width, length, axis=dim)
        leading = lax.slice_in_dim(value, 0, width, axis=dim)
        before = lax.ppermute(last, axis, up)
        after = lax.ppermute(leading, axis, down)
        value = jnp.concatenate([before, value, after], axis=dim)
    return value


def angles(count_rows, count_cols, modulus):
    row_ids = lax.broadcasted_iota(jnp.int32, (count_rows, count_cols), 0)
    col_ids = lax.broadcasted_iota(jnp.int32, (count_rows, count_cols), 1)
    phase = (row_ids * col_ids % modulus).astype(jnp.float32) * (2.0 * math.pi / modulus)
    return (jnp.cos(phase), jnp.sin(phase))


def fourier_tables(length):
    inner_len = min(128, length)
    padded_len = 2 * length
    outer_len = padded_len // inner_len
    cos_outer, sin_outer = angles(outer_len // 2, outer_len, outer_len)
    cos_twist, sin_twist = angles(outer_len, inner_len, padded_len)
    cos_inner, sin_inner = angles(inner_len, inner_len, inner_len)
    outer_fwd = jnp.stack([cos_outer, -sin_outer])
    inner_fwd = jnp.stack([jnp.stack([cos_inner, -sin_inner]), jnp.stack([sin_inner, cos_inner])])
    inner_inv = jnp.stack([jnp.stack([cos_inner, sin_inner]), jnp.stack([-sin_inner, cos_inner])])
    return (outer_fwd, cos_twist, sin_twist, inner_fwd, inner_inv, padded_len)


def forward(signal, tables):
    outer_fwd, cos_twist, sin_twist, inner_fwd, inner_inv, padded_len = tables
    shaped = signal.reshape(signal.shape[:-1] + (outer_fwd.shape[1], inner_fwd.shape[2]))
    first = jnp.einsum("...ab,caf->...cfb", shaped, outer_fwd, precision=precise)
    first_real = first[..., 0, :, :]
    first_imag = first[..., 1, :, :]
    twist = jnp.stack(
        [
            first_real * cos_twist + first_imag * sin_twist,
            first_imag * cos_twist - first_real * sin_twist,
        ],
        axis=-3,
    )
    return jnp.einsum("...cfb,cdbk->...dfk", twist, inner_fwd, precision=precise)


def inverse(spectrum, tables):
    outer_fwd, cos_twist, sin_twist, inner_fwd, inner_inv, padded_len = tables
    first = jnp.einsum("...cfk,cdkb->...dfb", spectrum, inner_inv, precision=precise)
    first_real = first[..., 0, :, :]
    first_imag = first[..., 1, :, :]
    twist = jnp.stack(
        [
            first_real * cos_twist - first_imag * sin_twist,
            first_imag * cos_twist + first_real * sin_twist,
        ],
        axis=-3,
    )
    result = jnp.einsum("...cfb,caf->...ab", twist, outer_fwd, precision=precise)
    result = result / padded_len
    return result.reshape(result.shape[:-2] + (result.shape[-2] * result.shape[-1],))


def on_device(queries, key_rows, value_rows, short_taps, long_filter):
    tokens = queries.shape[1]
    rim_width = TAPS - 1
    stacked = jnp.stack([queries, key_rows, value_rows])
    padded = with_halo(stacked, (("ctx", 2),), rim_width)
    mirrored_taps = short_taps[:, ::-1, :]
    causal = jnp.zeros(stacked.shape, jnp.float32)
    anticausal = jnp.zeros(stacked.shape, jnp.float32)
    for offset in range(TAPS):
        begin = rim_width - offset
        causal = causal + short_taps[:, :, offset, None] * padded[:, :, begin : begin + tokens]
        later = rim_width + offset
        anticausal = (
            anticausal + mirrored_taps[:, :, offset, None] * padded[:, :, later : later + tokens]
        )
    product_a = (causal[1] * causal[2]).astype(jnp.bfloat16)
    product_b = (anticausal[1] * anticausal[2]).astype(jnp.bfloat16)
    tables = fourier_tables(long_filter.shape[1])
    outgoing = jnp.stack([product_a, product_b[::-1]])
    channel_rows = lax.all_to_all(outgoing, "ctx", split_axis=1, concat_axis=2, tiled=True)
    filter_spec = forward(long_filter.astype(jnp.float32), tables)
    data_spec = forward(channel_rows.astype(jnp.float32), tables)
    filter_real = filter_spec[:, 0]
    filter_imag = filter_spec[:, 1]
    data_real = data_spec[:, :, 0]
    data_imag = data_spec[:, :, 1]
    first_real = filter_real * data_real[0] - filter_imag * data_imag[0]
    first_imag = filter_real * data_imag[0] + filter_imag * data_real[0]
    second_real = filter_real * data_real[1] + filter_imag * data_imag[1]
    second_imag = filter_real * data_imag[1] - filter_imag * data_real[1]
    spectrum = jnp.stack(
        [jnp.stack([first_real, first_imag], axis=1), jnp.stack([second_real, second_imag], axis=1)]
    )
    convolved = inverse(spectrum, tables).astype(jnp.bfloat16)
    token_rows = lax.all_to_all(convolved, "ctx", split_axis=2, concat_axis=1, tiled=True)
    mixed_b = token_rows[1][::-1]
    result = causal[0] * token_rows[0].astype(jnp.float32) + anticausal[0] * mixed_b.astype(
        jnp.float32
    )
    return result.astype(jnp.bfloat16)


def solution(mesh):
    placed = (
        P(None, ("grp", "ctx")),
        P(None, ("grp", "ctx")),
        P(None, ("grp", "ctx")),
        P(),
        P("ctx", None),
    )
    return jax.shard_map(
        on_device, mesh=mesh, in_specs=placed, out_specs=P(None, ("grp", "ctx")), check_vma=False
    )
```

profile of v0, /device:TPU:0, one launch (start us, length us, event | category | flops | bytes accessed | tf_op | source)
XLA Modules:
  0.0 102.4 jit_solution(13261690223920789769)
XLA Ops:
  0.0 1.3 %pad_maximum_fusion.2 = bf16[3,960,128]{2,1,0:T(8,128)(2,1)S(1)} fusion(bf16[1,960,128]{2,1,0:T(8,128)(2,1)} %bitcast.184, bf16[1,960,128]{2,1,0:T(8,128)(2,1)} %bitcast.188, bf16[1,960,128]{2,1,0:T(8,128)(2,1)} %bitcast.192), kind=kLoop, calls=%fused_computation.55 | loop fusion | flops 737280 | bytes 1474560 | tf_op jit(solution)/shard_map/stack | solution.py:83
  1.9 1.3 %collective-permute-start.1 = (bf16[3,960,6]{1,2,0:T(8,128)(2,1)S(1)}, bf16[3,960,6]{1,2,0:T(8,128)(2,1)S(1)}, u32[]{:S(2)}, u32[]{:S(2)}) collective-permute-start(bf16[3,960,6]{1,2,0:T(8,128)(2,1)S(1)} %copy.51), channel_id=1, source_target_pairs={{1,0},{2,1},{3,2},{4,3},{5,4},{6,5},{7,6},{8,7},{9,8},{10,9},{11,1... | collective-permute-start | bytes 103688 | tf_op jit(solution)/shard_map/ppermute | solution.py:22
  3.5 3.0 %collective-permute-start = (bf16[3,960,6]{1,2,0:T(8,128)(2,1)S(1)}, bf16[3,960,6]{1,2,0:T(8,128)(2,1)S(1)}, u32[]{:S(2)}, u32[]{:S(2)}) collective-permute-start(bf16[3,960,6]{1,2,0:T(8,128)(2,1)S(1)} %copy.47), channel_id=1, source_target_pairs={{0,1},{1,2},{2,3},{3,4},{4,5},{5,6},{6,7},{7,8},{8,9},{9,10},{10,1... | collective-permute-start | bytes 103688 | tf_op jit(solution)/shard_map/ppermute | solution.py:21
  18.7 1.2 %copy.52 = bf16[3,960,6]{2,1,0:T(8,128)(2,1)} copy(bf16[3,960,6]{1,2,0:T(8,128)(2,1)S(1)} %collective-permute-done.1) | data formatting | bytes 69120 | tf_op jit(solution)/shard_map/ppermute | solution.py:22
  19.9 2.5 %maximum_maximum_fusion = (bf16[3,960,134]{2,1,0:T(8,128)(2,1)S(1)}, bf16[3,960,134]{2,1,0:T(8,128)(2,1)S(1)}) fusion(bf16[1,960,128]{2,1,0:T(8,128)(2,1)S(1)} %bitcast.185, bf16[1,960,128]{2,1,0:T(8,128)(2,1)S(1)} %bitcast.189, bf16[1,960,128]{2,1,0:T(8,128)(2,1)S(1)} %bitcast.193, bf16[3,960,6]{2,1,0:T(8,128)(2,1)S(1)} %copy.48, bf16[3,960,6]{2,1,0:T(8,128)(2,1)} %copy.52), kind=kLoop, calls=%fused_computation.39 | loop fusion | flops 6174720 | bytes 2350080 | tf_op jit(solution)/shard_map/concatenate | solution.py:23
  22.6 4.5 %fusion.31 = f32[3,960,128]{2,1,0:T(8,128)S(1)} fusion(bf16[3,960,134]{2,1,0:T(8,128)(2,1)S(1)} %get-tuple-element.16, f32[3,960]{1,0:T(4,128)S(1)} %copy-done.13, f32[3,960]{1,0:T(4,128)S(1)} %copy-done.14, f32[3,960]{1,0:T(4,128)S(1)} %copy-done.17, f32[3,960]{1,0:T(4,128)S(1)} %copy-done.18, f32[3,960]{1,0:T(4,128)S(1)} %copy-done.15, ...), kind=kLoop, calls=%fused_computation.38 | loop fusion | flops 8110080 | bytes 6716160 | tf_op jit(solution)/shard_map/add | solution.py:93
  27.1 1.1 %copy-done = f32[3,960,128]{2,1,0:T(8,128)} copy-done((f32[3,960,128]{2,1,0:T(8,128)}, f32[3,960,128]{2,1,0:T(8,128)S(1)}, u32[]{:S(2)}) %copy-start) | copy-done | bytes 1474584
  29.0 4.3 %fusion.25 = f32[3,960,128]{2,1,0:T(8,128)S(1)} fusion(bf16[3,960,134]{2,1,0:T(8,128)(2,1)S(1)} %get-tuple-element.15, f32[3,960]{1,0:T(4,128)S(1)} %get-tuple-element.34, f32[3,960]{1,0:T(4,128)S(1)} %get-tuple-element.35, f32[3,960]{1,0:T(4,128)S(1)} %copy-done.11, f32[3,960]{1,0:T(4,128)S(1)} %copy-done.12, f32[3,960]{1,0:T(4,128)S(1)} %copy-done.9, ...), kind=kLoop, calls=%fused_computation.32 | loop fusion | flops 8110080 | bytes 6716160 | tf_op jit(solution)/shard_map/add | solution.py:90
  33.3 1.1 %copy-done.1 = f32[3,960,128]{2,1,0:T(8,128)} copy-done((f32[3,960,128]{2,1,0:T(8,128)}, f32[3,960,128]{2,1,0:T(8,128)S(1)}, u32[]{:S(2)}) %copy-start.1) | copy-done | bytes 1474584
  34.5 1.3 %copy.53 = bf16[2,960,128]{2,0,1:T(2,128)(2,1)} copy(bf16[2,960,128]{2,1,0:T(8,128)(2,1)S(1)} %pad_maximum_fusion.3) | data formatting | bytes 983040 | tf_op jit(solution)/shard_map/stack | solution.py:98
  35.8 8.1 %all-to-all-start = ((bf16[2,960,128]{2,0,1:T(2,128)(2,1)}), bf16[2,960,128]{2,0,1:T(2,128)(2,1)S(1)}, u32[]{:S(2)}, u32[]{:S(2)}) async-start(bf16[2,960,128]{2,0,1:T(2,128)(2,1)} %copy.53), calls=%async_computation | async-start | bytes 983040 | tf_op jit(solution)/shard_map/all_to_all | solution.py:99
  45.2 2.0 %fusion.17 = f32[60,2,32,128]{3,0,2,1:T(8,128)S(1)} fusion(f32[60,2,32,128]{3,2,0,1:T(8,128)S(1)} %pad_maximum_fusion, f32[1,2,128,128]{3,2,0,1:T(8,128)S(1)} %get-tuple-element.22, f32[1,2,128,128]{3,2,0,1:T(8,128)S(1)} %get-tuple-element.32), kind=kOutput, calls=%fused_computation.25 | convolution fusion | flops 755040256 | bytes 4194304 | tf_op jit(solution)/shard_map/...cfb,cdbk->...dfk/dot_general | solution.py:60
  47.2 10.4 %all-to-all-done = bf16[2,960,128]{2,0,1:T(2,128)(2,1)S(1)} async-done(((bf16[2,960,128]{2,0,1:T(2,128)(2,1)}), bf16[2,960,128]{2,0,1:T(2,128)(2,1)S(1)}, u32[]{:S(2)}, u32[]{:S(2)}) %all-to-all-start) | async-done | bytes 491552 | tf_op jit(solution)/shard_map/all_to_all | solution.py:99
  57.6 1.2 %convolution_bitcast_fusion = f32[2,60,2,32,128]{4,3,1,0,2:T(8,128)S(1)} fusion(bf16[2,16,60,128]{3,0,2,1:T(2,128)(2,1)S(1)} %bitcast.196, f32[1,16,32]{2,1,0:T(8,128)S(1)} %get-tuple-element.46, f32[1,16,32]{2,1,0:T(8,128)S(1)} %get-tuple-element.47), kind=kOutput, calls=%fused_computation.17 | convolution fusion | flops 94372864 | bytes 4427776 | tf_op jit(solution)/shard_map/...ab,caf->...cfb/dot_general | solution.py:50
  60.0 5.0 %fusion.8 = f32[2,60,2,32,128]{4,1,3,2,0:T(8,128)S(1)} fusion(f32[2,60,2,32,128,1]{4,3,1,0,2,5:T(8,128)S(1)} %maximum_bitcast_fusion.1, f32[1,2,128,128]{3,2,0,1:T(8,128)S(1)} %get-tuple-element.22, f32[1,2,128,128]{3,2,0,1:T(8,128)S(1)} %get-tuple-element.32), kind=kOutput, calls=%fused_computation.10 | convolution fusion | flops 1510014976 | bytes 8126464 | tf_op jit(solution)/shard_map/...cfb,cdbk->...dfk/dot_general | solution.py:60
  65.0 1.0 multiply_subtract_fusion.3
  67.3 4.5 %fusion.14 = f32[2,60,2,32,128]{4,3,1,0,2:T(8,128)S(1)} fusion(f32[2,60,2,32,128,1]{4,1,3,2,0,5:T(8,128)S(1)} %maximum_bitcast_fusion, f32[1,2,128,128]{3,2,1,0:T(8,128)S(1)} %copy-done.7, f32[1,2,128,128]{3,2,1,0:T(8,128)S(1)} %copy-done.6), kind=kOutput, calls=%fused_computation.16 | convolution fusion | flops 1510014976 | bytes 8126464 | tf_op jit(solution)/shard_map/...cfk,cdkb->...dfb/dot_general | solution.py:65
  72.4 1.3 %fusion.41 = bf16[2,60,16,128]{3,2,1,0:T(8,128)(2,1)S(1)} fusion(f32[2,60,1,32,128]{4,3,1,0,2:T(8,128)S(1)} %get-tuple-element.10, f32[2,60,1,32,128]{4,3,1,0,2:T(8,128)S(1)} %get-tuple-element.9, f32[1,16,32]{2,1,0:T(8,128)S(1)} %get-tuple-element.46, f32[1,16,32]{2,1,0:T(8,128)S(1)} %get-tuple-element.47), kind=kOutput, calls=%fused_computation.44 | convolution fusion | flops 95847424 | bytes 4427776 | tf_op jit(solution)/shard_map/...cfb,caf->...ab/dot_general | solution.py:75
  73.7 0.8 copy.89
  74.6 2.8 %reshape.225 = bf16[16,2,7680]{2,1,0:T(2,128)(2,1)S(1)} reshape(bf16[2048,2,60]{2,1,0:T(2,128)(2,1)S(1)} %bitcast.182) | data formatting | bytes 983040
  77.4 17.7 %all_to_all.30 = bf16[16,2,7680]{2,1,0:T(2,128)(2,1)S(1)} all-to-all(bf16[16,2,7680]{2,1,0:T(2,128)(2,1)S(1)} %reshape.225), channel_id=1, replica_groups=mesh['grp'=2,'ctx'=16] {'ctx'}, dimensions={0} | all-to-all | bytes 983040 | tf_op jit(solution)/shard_map/all_to_all | solution.py:114
  95.0 3.5 %reshape.226 = bf16[2048,2,60]{2,1,0:T(2,128)(2,1)S(1)} reshape(bf16[16,2,7680]{2,1,0:T(2,128)(2,1)S(1)} %all_to_all.30) | data formatting | bytes 983040
  98.6 0.8 copy.88
  100.4 2.0 %fusion.46 = bf16[960,128]{1,0:T(8,128)(2,1)} fusion(f32[3,960,128]{2,1,0:T(8,128)} %copy-done, f32[960,128]{1,0:T(8,128)S(1)} %reshape.208, f32[3,960,128]{2,1,0:T(8,128)} %copy-done.1, bf16[960,128]{1,0:T(8,128)(2,1)S(1)} %rev.8), kind=kLoop, calls=%fused_computation.59 | loop fusion | flops 614400 | bytes 1966080 | tf_op jit(solution)/shard_map/convert_element_type | solution.py:119
  (94 shorter events, 19.0 us)
Async XLA Ops:
  1.3 5.9 %copy-start.8 = (f32[3,960,7]{1,2,0:T(8,128)S(1)}, f32[3,960,7]{1,2,0:T(8,128)}, u32[]{:S(2)}) copy-start(f32[3,960,7]{1,2,0:T(8,128)} %param.8) | copy-start | bytes 241924
  1.6 16.6 %copy-start.5 = (bf16[60,2048]{1,0:T(8,128)(2,1)S(1)}, bf16[60,2048]{1,0:T(8,128)(2,1)}, u32[]{:S(2)}) copy-start(bf16[60,2048]{1,0:T(8,128)(2,1)} %param.9) | copy-start | bytes 737284
  1.9 16.8 %collective-permute-start.1 = (bf16[3,960,6]{1,2,0:T(8,128)(2,1)S(1)}, bf16[3,960,6]{1,2,0:T(8,128)(2,1)S(1)}, u32[]{:S(2)}, u32[]{:S(2)}) collective-permute-start(bf16[3,960,6]{1,2,0:T(8,128)(2,1)S(1)} %copy.51), channel_id=1, source_target_pairs={{1,0},{2,1},{3,2},{4,3},{5,4},{6,5},{7,6},{8,7},{9,8},{10,9},{11,1... | collective-permute-start | bytes 103688 | tf_op jit(solution)/shard_map/ppermute | solution.py:22
  3.5 14.7 %collective-permute-start = (bf16[3,960,6]{1,2,0:T(8,128)(2,1)S(1)}, bf16[3,960,6]{1,2,0:T(8,128)(2,1)S(1)}, u32[]{:S(2)}, u32[]{:S(2)}) collective-permute-start(bf16[3,960,6]{1,2,0:T(8,128)(2,1)S(1)} %copy.47), channel_id=1, source_target_pairs={{0,1},{1,2},{2,3},{3,4},{4,5},{5,6},{6,7},{7,8},{8,9},{9,10},{10,1... | collective-permute-start | bytes 103688 | tf_op jit(solution)/shard_map/ppermute | solution.py:21
  6.9 13.0 %copy-start.2 = (bf16[960,128]{1,0:T(8,128)(2,1)S(1)}, bf16[960,128]{1,0:T(8,128)(2,1)}, u32[]{:S(2)}) copy-start(bf16[960,128]{1,0:T(8,128)(2,1)} %param.7) | copy-start | bytes 737284
  6.9 13.0 %copy-start.3 = (bf16[960,128]{1,0:T(8,128)(2,1)S(1)}, bf16[960,128]{1,0:T(8,128)(2,1)}, u32[]{:S(2)}) copy-start(bf16[960,128]{1,0:T(8,128)(2,1)} %param.6) | copy-start | bytes 737284
  6.9 13.0 %copy-start.4 = (bf16[960,128]{1,0:T(8,128)(2,1)S(1)}, bf16[960,128]{1,0:T(8,128)(2,1)}, u32[]{:S(2)}) copy-start(bf16[960,128]{1,0:T(8,128)(2,1)} %param.5) | copy-start | bytes 737284
  19.9 2.6 %copy-start.13 = (f32[3,960]{1,0:T(4,128)S(1)}, f32[3,960]{1,0:T(4,128)}, u32[]{:S(2)}) copy-start(f32[3,960]{1,0:T(4,128)} %get-tuple-element.40) | copy-start | bytes 34564
  19.9 2.6 %copy-start.14 = (f32[3,960]{1,0:T(4,128)S(1)}, f32[3,960]{1,0:T(4,128)}, u32[]{:S(2)}) copy-start(f32[3,960]{1,0:T(4,128)} %get-tuple-element.41) | copy-start | bytes 34564
  19.9 2.6 %copy-start.15 = (f32[3,960]{1,0:T(4,128)S(1)}, f32[3,960]{1,0:T(4,128)}, u32[]{:S(2)}) copy-start(f32[3,960]{1,0:T(4,128)} %get-tuple-element.44) | copy-start | bytes 34564
  19.9 2.6 %copy-start.16 = (f32[3,960]{1,0:T(4,128)S(1)}, f32[3,960]{1,0:T(4,128)}, u32[]{:S(2)}) copy-start(f32[3,960]{1,0:T(4,128)} %get-tuple-element.45) | copy-start | bytes 34564
  19.9 2.6 %copy-start.17 = (f32[3,960]{1,0:T(4,128)S(1)}, f32[3,960]{1,0:T(4,128)}, u32[]{:S(2)}) copy-start(f32[3,960]{1,0:T(4,128)} %get-tuple-element.42) | copy-start | bytes 34564
  19.9 2.6 %copy-start.18 = (f32[3,960]{1,0:T(4,128)S(1)}, f32[3,960]{1,0:T(4,128)}, u32[]{:S(2)}) copy-start(f32[3,960]{1,0:T(4,128)} %get-tuple-element.43) | copy-start | bytes 34564
  19.9 2.6 %copy-start.20 = (f32[3,960,1]{1,0,2:T(4,128)S(1)}, f32[3,960,1]{1,0,2:T(4,128)}, u32[]{:S(2)}) copy-start(f32[3,960,1]{1,0,2:T(4,128)} %copy.139) | copy-start | bytes 34564
  22.5 6.4 %copy-start.9 = (f32[3,960]{1,0:T(4,128)S(1)}, f32[3,960]{1,0:T(4,128)}, u32[]{:S(2)}) copy-start(f32[3,960]{1,0:T(4,128)} %get-tuple-element.38) | copy-start | bytes 34564
  22.5 6.4 %copy-start.10 = (f32[3,960]{1,0:T(4,128)S(1)}, f32[3,960]{1,0:T(4,128)}, u32[]{:S(2)}) copy-start(f32[3,960]{1,0:T(4,128)} %get-tuple-element.39) | copy-start | bytes 34564
  22.6 6.4 %copy-start.11 = (f32[3,960]{1,0:T(4,128)S(1)}, f32[3,960]{1,0:T(4,128)}, u32[]{:S(2)}) copy-start(f32[3,960]{1,0:T(4,128)} %get-tuple-element.36) | copy-start | bytes 34564
  22.6 6.4 %copy-start.12 = (f32[3,960]{1,0:T(4,128)S(1)}, f32[3,960]{1,0:T(4,128)}, u32[]{:S(2)}) copy-start(f32[3,960]{1,0:T(4,128)} %get-tuple-element.37) | copy-start | bytes 34564
  22.6 6.4 %copy-start.19 = (f32[3,960,1]{1,0,2:T(4,128)S(1)}, f32[3,960,1]{1,0,2:T(4,128)}, u32[]{:S(2)}) copy-start(f32[3,960,1]{1,0,2:T(4,128)} %copy.140) | copy-start | bytes 34564
  27.1 1.1 %copy-start = (f32[3,960,128]{2,1,0:T(8,128)}, f32[3,960,128]{2,1,0:T(8,128)S(1)}, u32[]{:S(2)}) copy-start(f32[3,960,128]{2,1,0:T(8,128)S(1)} %fusion.31) | copy-start | bytes 4423684
  33.3 1.1 %copy-start.1 = (f32[3,960,128]{2,1,0:T(8,128)}, f32[3,960,128]{2,1,0:T(8,128)S(1)}, u32[]{:S(2)}) copy-start(f32[3,960,128]{2,1,0:T(8,128)S(1)} %fusion.25) | copy-start | bytes 4423684
  35.8 21.7 %all-to-all-start = ((bf16[2,960,128]{2,0,1:T(2,128)(2,1)}), bf16[2,960,128]{2,0,1:T(2,128)(2,1)S(1)}, u32[]{:S(2)}, u32[]{:S(2)}) async-start(bf16[2,960,128]{2,0,1:T(2,128)(2,1)} %copy.53), calls=%async_computation | async-start | bytes 983040 | tf_op jit(solution)/shard_map/all_to_all | solution.py:99
  66.3 0.9 copy-start.6
  66.4 1.0 copy-start.7
where the time goes:
time: 103 us; the launch traced here: 102 us
  local copies, waits for them, and re-layouts  26.3 us (26%)
  other arithmetic  20.2 us (20%)
  blocking collectives  17.7 us (17%)
  matrix products  14.7 us (14%)
  starting transfers between devices  12.5 us (12%)
  waiting for transfers between devices  10.4 us (10%)
    unnamed x67, local copies, waits for them, and re-layouts  19.2 us
    all_to_all x1, blocking collectives, on_device(): lax.all_to_all(convolved, 'ctx', split_axis=2, concat_axis=1, tiled=True)  17.7 us
    all_to_all x1, waiting for transfers between devices, on_device(): lax.all_to_all(outgoing, 'ctx', split_axis=1, concat_axis=2, tiled=True)  10.4 us
    all_to_all x1, starting transfers between devices, on_device(): lax.all_to_all(outgoing, 'ctx', split_axis=1, concat_axis=2, tiled=True)  8.13 us
    dot_general x2, matrix products, forward(): jnp.einsum('...cfb,cdbk->...dfk', twist, inner_fwd, precision=precise)  6.97 us
    add x1, other arithmetic, on_device(): anticausal + mirrored_taps[:, :, offset, None] * padded[:, :, later:later...  4.54 us
    dot_general x1, matrix products, inverse(): jnp.einsum('...cfk,cdkb->...dfb', spectrum, inner_inv, precision=precise)  4.47 us
    add x1, other arithmetic, on_device(): causal + short_taps[:, :, offset, None] * padded[:, :, begin:begin + tokens]  4.31 us
  transfers between devices with their start and end apart: 3, of which 1 were waited for; matrix products, arithmetic and copies ran while one was open for 15% of the time, Pallas kernels for 0%

commit v1 on v0

v1 whole, which is shorter than its diff:
```python
import functools

import jax
import jax.numpy as jnp
from jax import lax
from jax.experimental import pallas as pl
from jax.experimental.pallas import tpu as pltpu
from jax.sharding import PartitionSpec as P

TAPS = 7
LANES = 128
F32 = jnp.float32
BF16 = jnp.bfloat16


def dims_of(cblk):
    cpad = -(-cblk // 16) * 16
    low = (cpad - cblk) // 2
    rows = 32 if cpad % 32 == 0 and 2 * low + cblk == cpad else cpad
    return cpad, low, rows


def unit(flip):
    i = lax.broadcasted_iota(jnp.int32, (LANES, LANES), 0)
    j = lax.broadcasted_iota(jnp.int32, (LANES, LANES), 1)
    j = LANES - 1 - j if flip else j
    return (i == j).astype(F32).astype(BF16)


def to_time_major(mat, x):
    return lax.dot_general(mat, x, (((1,), (1,)), ((), ())), preferred_element_type=F32)


def to_channel_major(x, mat):
    return lax.dot_general(x, mat, (((0,), (0,)), ((), ())), preferred_element_type=F32)


def short_sum(xs, taps, way, which, lanes):
    total = None
    for j in range(TAPS):
        start = 8 - j if way == 0 else 8 + j
        term = taps[way, which, j : j + 1, lanes] * xs[which, start : start + LANES, lanes]
        total = term if total is None else total + term
    return total


def kernel(
    n, cblk, x_ref, taps, filt, out,
    xs, qmix, snd, rcv, osnd, orcv, h32, xfa, xfb, ya, yb, toep, lhs,
    hs_sem, hr_sem, s_sem, r_sem, os_sem, or_sem,
):
    cpad, low, rows = dims_of(cblk)
    nch = cpad // rows
    cp = n * cpad
    me = lax.axis_index("ctx")
    groups = cp // LANES
    per = LANES // cpad

    barrier = pltpu.get_barrier_semaphore()

    def greet(o, carry):
        pl.semaphore_signal(barrier, inc=1, device_id={"ctx": lax.rem(me + o, n)})
        return carry

    lax.fori_loop(1, n, greet, 0)

    eye = unit(False)
    flip = unit(True)
    for a in range(3):
        for g in range(groups):
            ls = slice(g * LANES, (g + 1) * LANES)
            xs[a, 8 : 8 + LANES, ls] = to_time_major(eye, x_ref[a, ls, :])

    pl.semaphore_wait(barrier, n - 1)

    def halo(a, up):
        if up:
            return pltpu.make_async_remote_copy(
                src_ref=xs.at[a, pl.ds(LANES, 8)], dst_ref=xs.at[a, pl.ds(0, 8)],
                send_sem=hs_sem.at[0, a], recv_sem=hr_sem.at[0, a],
                device_id={"ctx": lax.rem(me + 1, n)},
            )
        return pltpu.make_async_remote_copy(
            src_ref=xs.at[a, pl.ds(8, 8)], dst_ref=xs.at[a, pl.ds(8 + LANES, 8)],
            send_sem=hs_sem.at[1, a], recv_sem=hr_sem.at[1, a],
            device_id={"ctx": lax.rem(me + n - 1, n)},
        )

    @pl.when(me < n - 1)
    def _():
        for a in (1, 2, 0):
            halo(a, True).start()

    @pl.when(me > 0)
    def _():
        for a in (1, 2, 0):
            halo(a, False).start()

    @pl.when(me == 0)
    def _():
        xs[:, 0:8, :] = jnp.zeros((3, 8, cp), F32)

    @pl.when(me == n - 1)
    def _():
        xs[:, 8 + LANES : 16 + LANES, :] = jnp.zeros((3, 8, cp), F32)

    for d in range(n):
        h32[d] = filt[:, d * LANES : (d + 1) * LANES].astype(F32)
    xfa[0 : n * rows, :] = jnp.zeros((n * rows, LANES), F32)
    xfb[0 : n * rows, :] = jnp.zeros((n * rows, LANES), F32)

    def halo_wait(arrays):
        @pl.when(me > 0)
        def _():
            for a in arrays:
                halo(a, True).wait_recv()

        @pl.when(me < n - 1)
        def _():
            for a in arrays:
                halo(a, False).wait_recv()

    halo_wait((1, 2))
    for g in range(groups):
        ls = slice(g * LANES, (g + 1) * LANES)
        pa = (short_sum(xs, taps, 0, 1, ls) * short_sum(xs, taps, 0, 2, ls)).astype(BF16)
        pb = (short_sum(xs, taps, 1, 1, ls) * short_sum(xs, taps, 1, 2, ls)).astype(BF16)
        pa = to_channel_major(pa, eye).astype(BF16)
        pb = to_channel_major(pb, flip).astype(BF16)
        for s in range(per):
            block = g * per + s
            for m in range(nch):
                part = slice(s * cpad + m * rows, s * cpad + (m + 1) * rows)
                snd[m, block, 0] = pa[part]
                snd[nch - 1 - m, n - 1 - block, 1] = pb[part]

    def data_copy(m, dest, slot):
        return pltpu.make_async_remote_copy(
            src_ref=snd.at[m, dest], dst_ref=rcv.at[m, slot],
            send_sem=s_sem.at[m, dest], recv_sem=r_sem.at[m, slot],
            device_id={"ctx": dest},
        )

    def back_copy(m, dest, slot):
        return pltpu.make_async_remote_copy(
            src_ref=osnd.at[m, dest], dst_ref=orcv.at[m, slot],
            send_sem=os_sem.at[m, dest], recv_sem=or_sem.at[m, slot],
            device_id={"ctx": dest},
        )

    def each_peer(act):
        def step(o, carry):
            act(lax.rem(me + o, n))
            return carry

        lax.fori_loop(1, n, step, 0)

    for m in range(nch):
        each_peer(lambda peer: data_copy(m, peer, me).start())

    halo_wait((0,))
    for g in range(groups):
        ls = slice(g * LANES, (g + 1) * LANES)
        qmix[0, :, ls] = short_sum(xs, taps, 0, 0, ls)
        qmix[1, :, ls] = short_sum(xs, taps, 1, 0, ls)

    row_id = lax.broadcasted_iota(jnp.int32, (LANES, LANES), 0)
    col_id = lax.broadcasted_iota(jnp.int32, (LANES, LANES), 1)
    causal = col_id >= row_id

    for m in range(nch):
        each_peer(lambda peer: data_copy(m, me, peer).wait_recv())
        rcv[m, me] = snd[m, me]

        def widen(src, carry):
            at = pl.multiple_of((n + src) * rows, rows)
            xfa[pl.ds(at, rows), :] = rcv[m, src, 0].astype(F32)
            at = pl.multiple_of((n + n - 1 - src) * rows, rows)
            xfb[pl.ds(at, rows), :] = rcv[m, src, 1].astype(F32)
            return carry

        lax.fori_loop(0, n, widen, 0, unroll=4)

        first = max(m * rows, low)
        last = min((m + 1) * rows, low + cblk)

        def channel(p, carry):
            row_a = p - m * rows
            row_b = 2 * low + cblk - 1 - p - (nch - 1 - m) * rows
            row_h = p - low

            def fill(d, before):
                at = d * LANES
                if not isinstance(d, int):
                    at = pl.multiple_of(at, LANES)
                line = h32[d, pl.ds(row_h, 1), :]
                turned = pltpu.roll(
                    jnp.broadcast_to(line, (LANES, LANES)), 0, 1, stride=1, stride_axis=0
                )
                toep[pl.ds(at, LANES), :] = jnp.where(causal, turned, before).astype(BF16)
                xa = xfa[pl.ds((n - d) * rows + row_a, n, stride=rows), :]
                xb = xfb[pl.ds((n - d) * rows + row_b, n, stride=rows), :]
                lhs[:, pl.ds(at, LANES)] = jnp.concatenate([xa, xb], axis=0).astype(BF16)
                return turned

            start = jnp.zeros((LANES, LANES), F32)
            if n <= 16:
                for d in range(n):
                    start = fill(d, start)
            else:
                lax.fori_loop(0, n, fill, start)
            y = jnp.dot(lhs[...], toep[...], preferred_element_type=F32)
            ya[pl.ds(row_a, n, stride=rows), :] = y[:n]
            yb[pl.ds(row_b, n, stride=rows), :] = y[n:]
            return carry

        lax.fori_loop(first, last, channel, 0)

        def narrow(dest, carry):
            at = pl.multiple_of(dest * rows, rows)
            osnd[m, dest, 0] = ya[pl.ds(at, rows), :].astype(BF16)
            at = pl.multiple_of((n - 1 - dest) * rows, rows)
            osnd[m, dest, 1] = yb[pl.ds(at, rows), :].astype(BF16)
            return carry

        lax.fori_loop(0, n, narrow, 0, unroll=4)
        each_peer(lambda peer: back_copy(m, peer, me).start())
        orcv[m, me] = osnd[m, me]

    for m in range(nch):
        each_peer(lambda peer: back_copy(m, me, peer).wait_recv())

    for g in range(groups):
        ls = slice(g * LANES, (g + 1) * LANES)
        blocks = [g * per + s for s in range(per)]
        ma = jnp.concatenate([orcv[m, b, 0] for b in blocks for m in range(nch)], axis=0)
        mb = jnp.concatenate(
            [orcv[nch - 1 - m, n - 1 - b, 1] for b in blocks for m in range(nch)], axis=0
        )
        mixed = qmix[0, :, ls] * to_time_major(eye, ma) + qmix[1, :, ls] * to_time_major(flip, mb)
        out[ls, :] = to_channel_major(mixed.astype(BF16), eye).astype(BF16)

    for m in range(nch):
        each_peer(lambda peer: data_copy(m, peer, me).wait_send())
        each_peer(lambda peer: back_copy(m, peer, me).wait_send())

    @pl.when(me < n - 1)
    def _():
        for a in range(3):
            halo(a, True).wait_send()

    @pl.when(me > 0)
    def _():
        for a in range(3):
            halo(a, False).wait_send()


def on_device(queries, key_rows, value_rows, short_taps, long_filter):
    n = lax.axis_size("ctx")
    channels, tokens = queries.shape
    cblk, length = long_filter.shape
    cpad, low, rows = dims_of(cblk)
    nch = cpad // rows
    cp = n * cpad
    pad = ((0, 0), (0, 0), (low, cpad - cblk - low), (0, 0))
    x = jnp.stack([queries, key_rows, value_rows]).reshape(3, n, cblk, tokens)
    x = jnp.pad(x, pad).reshape(3, cp, tokens)
    taps = jnp.stack([short_taps, short_taps[:, ::-1, :]]).reshape(6, n, cblk, TAPS)
    taps = jnp.pad(taps, pad).reshape(2, 3, cp, TAPS)
    taps = jnp.pad(jnp.swapaxes(taps, 2, 3), ((0, 0), (0, 0), (0, 1), (0, 0)))
    vmem = pl.BlockSpec(memory_space=pltpu.VMEM)
    dma = pltpu.SemaphoreType.DMA
    mixed = pl.pallas_call(
        functools.partial(kernel, n, cblk),
        out_shape=jax.ShapeDtypeStruct((cp, tokens), BF16),
        in_specs=[vmem] * 3,
        out_specs=vmem,
        scratch_shapes=[
            pltpu.VMEM((3, LANES + 16, cp), F32),
            pltpu.VMEM((2, LANES, cp), F32),
            pltpu.VMEM((nch, n, 2, rows, LANES), BF16),
            pltpu.VMEM((nch, n, 2, rows, LANES), BF16),
            pltpu.VMEM((nch, n, 2, rows, LANES), BF16),
            pltpu.VMEM((nch, n, 2, rows, LANES), BF16),
            pltpu.VMEM((n, cblk, LANES), F32),
            pltpu.VMEM((2 * n * rows, LANES), F32),
            pltpu.VMEM((2 * n * rows, LANES), F32),
            pltpu.VMEM((n * rows, LANES), F32),
            pltpu.VMEM((n * rows, LANES), F32),
            pltpu.VMEM((length, LANES), BF16),
            pltpu.VMEM((2 * n, length), BF16),
            dma((2, 3)),
            dma((2, 3)),
            dma((nch, n)),
            dma((nch, n)),
            dma((nch, n)),
            dma((nch, n)),
        ],
        compiler_params=pltpu.CompilerParams(
            collective_id=0, has_side_effects=True, vmem_limit_bytes=48 * 1024 * 1024
        ),
    )(x, taps, long_filter)
    mixed = mixed.reshape(n, cpad, tokens)[:, low : low + cblk]
    return mixed.reshape(channels, tokens)


def solution(mesh):
    placed = (
        P(None, ("grp", "ctx")),
        P(None, ("grp", "ctx")),
        P(None, ("grp", "ctx")),
        P(),
        P("ctx", None),
    )
    return jax.shard_map(
        on_device, mesh=mesh, in_specs=placed, out_specs=P(None, ("grp", "ctx")), check_vma=False
    )
```

time: 103 us -> 67.9 us (0.66)
  Pallas kernels: 0 us -> 61.9 us
  local copies, waits for them, and re-layouts: 26.3 us -> 5.33 us
  other arithmetic: 20.2 us -> 0.35 us
  blocking collectives: 17.7 us -> 0 us
  matrix products: 14.7 us -> 0 us
  starting transfers between devices: 12.5 us -> 0 us
  waiting for transfers between devices: 10.4 us -> 0 us
    pallas_call x0 -> x1, Pallas kernels: none -> 61.9 us  [on_device(): pl.pallas_call(functools.partial(kernel, n, cblk), out_shape=jax.ShapeDty...]
    all_to_all x1 -> x0, blocking collectives: 17.7 us -> none  [on_device(): lax.all_to_all(convolved, 'ctx', split_axis=2, concat_axis=1, tiled=True)]
    unnamed x67 -> x7, local copies, waits for them, and re-layouts: 19.2 us -> 1.76 us
    dot_general x6 -> x0, matrix products: 14.7 us -> none  [the longest x2 6.97 us: forward(): jnp.einsum('...cfb,cdbk->...dfk', twist, inner_fwd, precision=precise)]
    all_to_all x1 -> x0, waiting for transfers between devices: 10.4 us -> none  [on_device(): lax.all_to_all(outgoing, 'ctx', split_axis=1, concat_axis=2, tiled=True)]
    add x4 -> x0, other arithmetic: 9.96 us -> none  [the longest x1 4.54 us: on_device(): anticausal + mirrored_taps[:, :, offset, None] * padded[:, :, later:later...]
    all_to_all x1 -> x0, starting transfers between devices: 8.13 us -> none  [on_device(): lax.all_to_all(outgoing, 'ctx', split_axis=1, concat_axis=2, tiled=True)]
    ppermute x2 -> x0, starting transfers between devices: 4.33 us -> none  [the longest x1 3.03 us: with_halo(): before = lax.ppermute(last, axis, up)]
  transfers between devices with their start and end apart: 3 -> 0, of which waited for: 1 -> 0; matrix products, arithmetic and copies ran while one was open for 15% -> 0% of each run, Pallas kernels for 0% -> 0%
where the time goes in v1:
time: 67.9 us; the launch traced here: 67.7 us
  Pallas kernels  61.9 us (91%)
  local copies, waits for them, and re-layouts  5.33 us (8%)
    pallas_call x1, Pallas kernels, on_device(): pl.pallas_call(functools.partial(kernel, n, cblk), out_shape=jax.ShapeDty...  61.9 us
    another operation x3, local copies, waits for them, and re-layouts, on_device(): x = jnp.stack([queries, key_rows, value_rows]).reshape(3, n, cblk, tokens)  2.07 us
    unnamed x7, local copies, waits for them, and re-layouts  1.76 us

profile of v1, /device:TPU:0, one launch (start us, length us, event | category | flops | bytes accessed | tf_op | source)
XLA Modules:
  0.0 67.7 jit_solution(87420501768765732)
XLA Ops:
  0.0 0.0 copy-start.2
  0.0 1.0 %stack.21 = bf16[1,16,60,128]{3,2,1,0:T(8,128)(2,1)S(1)} reshape(bf16[960,128]{1,0:T(8,128)(2,1)} %param.5) | data formatting | bytes 491520 | tf_op jit(solution)/shard_map/stack | solution.py:266
  1.0 1.0 %stack.22 = bf16[1,16,60,128]{3,2,1,0:T(8,128)(2,1)S(1)} reshape(bf16[960,128]{1,0:T(8,128)(2,1)} %param.6) | data formatting | bytes 491520 | tf_op jit(solution)/shard_map/stack | solution.py:266
  2.0 0.0 copy-done.2
  2.1 0.0 copy-start.1
  2.1 0.3 fusion.5
  2.4 0.6 copy-done.1
  3.0 0.6 reverse
  3.6 0.1 slice_bitcast_fusion
  3.7 0.3 reshape.23
  4.0 0.0 copy-start
  4.0 0.1 pad.13
  4.2 0.1 reshape.24
  4.3 0.6 copy-done
  5.0 61.9 %shard_map.55 = bf16[1024,128]{1,0:T(8,128)(2,1)S(1)} custom-call(bf16[3,1024,128]{2,1,0:T(8,128)(2,1)S(1)} %bitcast.13, f32[2,3,8,1024]{3,2,1,0:T(8,128)S(1)} %pad.14.taps, bf16[60,2048]{1,0:T(8,128)(2,1)S(1)} %copy-done), custom_call_target="tpu_custom_call" | custom-call | tf_op jit(solution)/shard_map/pallas_call | solution.py:273
  66.8 0.1 slice.4
  66.9 0.7 %reshape.26 = bf16[960,128]{1,0:T(8,128)(2,1)} reshape(bf16[16,60,128]{2,1,0:T(8,128)(2,1)S(1)} %slice.4) | data formatting | bytes 491520 | tf_op jit(solution)/shard_map/reshape | solution.py:304
  (3 shorter events, 0.1 us)
Async XLA Ops:
  0.0 2.0 %copy-start.2 = (bf16[960,128]{1,0:T(8,128)(2,1)S(1)}, bf16[960,128]{1,0:T(8,128)(2,1)}, u32[]{:S(2)}) copy-start(bf16[960,128]{1,0:T(8,128)(2,1)} %param.7) | copy-start | bytes 737284
  2.1 0.9 %copy-start.1 = (f32[3,960,7]{1,2,0:T(8,128)S(1)}, f32[3,960,7]{1,2,0:T(8,128)}, u32[]{:S(2)}) copy-start(f32[3,960,7]{1,2,0:T(8,128)} %param.8) | copy-start | bytes 241924
  4.0 1.0 %copy-start = (bf16[60,2048]{1,0:T(8,128)(2,1)S(1)}, bf16[60,2048]{1,0:T(8,128)(2,1)}, u32[]{:S(2)}) copy-start(bf16[60,2048]{1,0:T(8,128)(2,1)} %filt.1) | copy-start | bytes 737284

commit v2 on v1

--- a/solution.py
+++ b/solution.py
@@ -46,13 +46,14 @@
 
 def kernel(
     n, cblk, x_ref, taps, filt, out,
-    xs, qmix, snd, rcv, osnd, orcv, h32, xfa, xfb, ya, yb, toep, lhs,
+    xs, qmix, snd, rcv, osnd, orcv, h32, xfa, xfb, ya, yb, toep0, toep1, lhs0, lhs1, xc0, xc1,
     hs_sem, hr_sem, s_sem, r_sem, os_sem, or_sem,
 ):
     cpad, low, rows = dims_of(cblk)
     nch = cpad // rows
     cp = n * cpad
     me = lax.axis_index("ctx")
+    toep, lhs, xc = (toep0, toep1), (lhs0, lhs1), (xc0, xc1)
     groups = cp // LANES
     per = LANES // cpad
 
@@ -106,8 +107,8 @@
 
     for d in range(n):
         h32[d] = filt[:, d * LANES : (d + 1) * LANES].astype(F32)
-    xfa[0 : n * rows, :] = jnp.zeros((n * rows, LANES), F32)
-    xfb[0 : n * rows, :] = jnp.zeros((n * rows, LANES), F32)
+    for half in range(2):
+        xc[half][:, 0:n, :] = jnp.zeros((2, n, LANES), F32)
 
     def halo_wait(arrays):
         @pl.when(me > 0)
@@ -173,9 +174,9 @@
         rcv[m, me] = snd[m, me]
 
         def widen(src, carry):
-            at = pl.multiple_of((n + src) * rows, rows)
+            at = pl.multiple_of(src * rows, rows)
             xfa[pl.ds(at, rows), :] = rcv[m, src, 0].astype(F32)
-            at = pl.multiple_of((n + n - 1 - src) * rows, rows)
+            at = pl.multiple_of((n - 1 - src) * rows, rows)
             xfb[pl.ds(at, rows), :] = rcv[m, src, 1].astype(F32)
             return carry
 
@@ -184,10 +185,15 @@
         first = max(m * rows, low)
         last = min((m + 1) * rows, low + cblk)
 
-        def channel(p, carry):
+        count = last - first
+
+        def build(p, half):
             row_a = p - m * rows
             row_b = 2 * low + cblk - 1 - p - (nch - 1 - m) * rows
             row_h = p - low
+            line_x = xc[half]
+            line_x[0, n : 2 * n, :] = xfa[pl.ds(row_a, n, stride=rows), :]
+            line_x[1, n : 2 * n, :] = xfb[pl.ds(row_b, n, stride=rows), :]
 
             def fill(d, before):
                 at = d * LANES
@@ -197,10 +203,10 @@
                 turned = pltpu.roll(
                     jnp.broadcast_to(line, (LANES, LANES)), 0, 1, stride=1, stride_axis=0
                 )
-                toep[pl.ds(at, LANES), :] = jnp.where(causal, turned, before).astype(BF16)
-                xa = xfa[pl.ds((n - d) * rows + row_a, n, stride=rows), :]
-                xb = xfb[pl.ds((n - d) * rows + row_b, n, stride=rows), :]
-                lhs[:, pl.ds(at, LANES)] = jnp.concatenate([xa, xb], axis=0).astype(BF16)
+                toep[half][pl.ds(at, LANES), :] = jnp.where(causal, turned, before).astype(BF16)
+                xa = line_x[0, pl.ds(n - d, n), :]
+                xb = line_x[1, pl.ds(n - d, n), :]
+                lhs[half][:, pl.ds(at, LANES)] = jnp.concatenate([xa, xb], axis=0).astype(BF16)
                 return turned
 
             start = jnp.zeros((LANES, LANES), F32)
@@ -209,12 +215,25 @@
                     start = fill(d, start)
             else:
                 lax.fori_loop(0, n, fill, start)
-            y = jnp.dot(lhs[...], toep[...], preferred_element_type=F32)
+
+        def apply(p, half):
+            row_a = p - m * rows
+            row_b = 2 * low + cblk - 1 - p - (nch - 1 - m) * rows
+            y = jnp.dot(lhs[half][...], toep[half][...], preferred_element_type=F32)
             ya[pl.ds(row_a, n, stride=rows), :] = y[:n]
             yb[pl.ds(row_b, n, stride=rows), :] = y[n:]
+
+        def pair(i, carry):
+            build(first + 2 * i + 1, 1)
+            apply(first + 2 * i, 0)
+            build(first + lax.rem(2 * i + 2, count), 0)
+            apply(first + 2 * i + 1, 1)
             return carry
 
-        lax.fori_loop(first, last, channel, 0)
+        build(first, 0)
+        lax.fori_loop(0, count // 2, pair, 0)
+        if count % 2:
+            apply(last - 1, 0)
 
         def narrow(dest, carry):
             at = pl.multiple_of(dest * rows, rows)
@@ -283,12 +302,16 @@
             pltpu.VMEM((nch, n, 2, rows, LANES), BF16),
             pltpu.VMEM((nch, n, 2, rows, LANES), BF16),
             pltpu.VMEM((n, cblk, LANES), F32),
-            pltpu.VMEM((2 * n * rows, LANES), F32),
-            pltpu.VMEM((2 * n * rows, LANES), F32),
+            pltpu.VMEM((n * rows, LANES), F32),
+            pltpu.VMEM((n * rows, LANES), F32),
             pltpu.VMEM((n * rows, LANES), F32),
             pltpu.VMEM((n * rows, LANES), F32),
             pltpu.VMEM((length, LANES), BF16),
+            pltpu.VMEM((length, LANES), BF16),
             pltpu.VMEM((2 * n, length), BF16),
+            pltpu.VMEM((2 * n, length), BF16),
+            pltpu.VMEM((2, 2 * n, LANES), F32),
+            pltpu.VMEM((2, 2 * n, LANES), F32),
             dma((2, 3)),
             dma((2, 3)),
             dma((nch, n)),

time: 67.9 us -> 50.3 us (0.74)
  Pallas kernels: 61.9 us -> 44.3 us
    pallas_call x1, Pallas kernels: 61.9 us -> 44.3 us  [on_device(): pl.pallas_call(functools.partial(kernel, n, cblk), out_shape=jax.ShapeDty...]
where the time goes in v2:
time: 50.3 us; the launch traced here: 50.1 us
  Pallas kernels  44.3 us (88%)
  local copies, waits for them, and re-layouts  5.33 us (11%)
    pallas_call x1, Pallas kernels, on_device(): pl.pallas_call(functools.partial(kernel, n, cblk), out_shape=jax.ShapeDty...  44.3 us
    another operation x3, local copies, waits for them, and re-layouts, on_device(): x = jnp.stack([queries, key_rows, value_rows]).reshape(3, n, cblk, tokens)  2.07 us
    unnamed x7, local copies, waits for them, and re-layouts  1.76 us

profile of v2, /device:TPU:0, one launch (start us, length us, event | category | flops | bytes accessed | tf_op | source)
XLA Modules:
  0.0 50.1 jit_solution(7253672484508678055)
XLA Ops:
  0.0 0.0 copy-start.2
  0.0 1.0 %stack.21 = bf16[1,16,60,128]{3,2,1,0:T(8,128)(2,1)S(1)} reshape(bf16[960,128]{1,0:T(8,128)(2,1)} %param.5) | data formatting | bytes 491520 | tf_op jit(solution)/shard_map/stack | solution.py:285
  1.0 1.0 %stack.22 = bf16[1,16,60,128]{3,2,1,0:T(8,128)(2,1)S(1)} reshape(bf16[960,128]{1,0:T(8,128)(2,1)} %param.6) | data formatting | bytes 491520 | tf_op jit(solution)/shard_map/stack | solution.py:285
  2.0 0.0 copy-done.2
  2.1 0.0 copy-start.1
  2.1 0.3 fusion.5
  2.4 0.6 %copy-done.1 = f32[3,960,7]{1,2,0:T(8,128)S(1)} copy-done((f32[3,960,7]{1,2,0:T(8,128)S(1)}, f32[3,960,7]{1,2,0:T(8,128)}, u32[]{:S(2)}) %copy-start.1) | copy-done | bytes 80664
  3.0 0.6 %reverse = f32[3,1024,7]{1,2,0:T(8,128)S(1)} reverse(f32[3,1024,7]{1,2,0:T(8,128)S(1)} %bitcast.16), dimensions={1} | reverse | bytes 172032
  3.6 0.1 slice_bitcast_fusion
  3.7 0.3 reshape.23
  4.0 0.0 copy-start
  4.0 0.1 pad.13
  4.2 0.1 reshape.24
  4.3 0.6 %copy-done = bf16[60,2048]{1,0:T(8,128)(2,1)S(1)} copy-done((bf16[60,2048]{1,0:T(8,128)(2,1)S(1)}, bf16[60,2048]{1,0:T(8,128)(2,1)}, u32[]{:S(2)}) %copy-start) | copy-done | bytes 245784
  5.0 44.3 %shard_map.55 = bf16[1024,128]{1,0:T(8,128)(2,1)S(1)} custom-call(bf16[3,1024,128]{2,1,0:T(8,128)(2,1)S(1)} %bitcast.13, f32[2,3,8,1024]{3,2,1,0:T(8,128)S(1)} %pad.14.taps, bf16[60,2048]{1,0:T(8,128)(2,1)S(1)} %copy-done), custom_call_target="tpu_custom_call" | custom-call | tf_op jit(solution)/shard_map/pallas_call | solution.py:292
  49.3 0.1 slice.4
  49.3 0.7 %reshape.26 = bf16[960,128]{1,0:T(8,128)(2,1)} reshape(bf16[16,60,128]{2,1,0:T(8,128)(2,1)S(1)} %slice.4) | data formatting | bytes 491520 | tf_op jit(solution)/shard_map/reshape | solution.py:327
  (3 shorter events, 0.1 us)
Async XLA Ops:
  0.0 2.0 %copy-start.2 = (bf16[960,128]{1,0:T(8,128)(2,1)S(1)}, bf16[960,128]{1,0:T(8,128)(2,1)}, u32[]{:S(2)}) copy-start(bf16[960,128]{1,0:T(8,128)(2,1)} %param.7) | copy-start | bytes 737284
  2.1 0.9 %copy-start.1 = (f32[3,960,7]{1,2,0:T(8,128)S(1)}, f32[3,960,7]{1,2,0:T(8,128)}, u32[]{:S(2)}) copy-start(f32[3,960,7]{1,2,0:T(8,128)} %param.8) | copy-start | bytes 241924
  4.0 1.0 %copy-start = (bf16[60,2048]{1,0:T(8,128)(2,1)S(1)}, bf16[60,2048]{1,0:T(8,128)(2,1)}, u32[]{:S(2)}) copy-start(bf16[60,2048]{1,0:T(8,128)(2,1)} %filt.1) | copy-start | bytes 737284

commit v3 on v2

--- a/solution.py
+++ b/solution.py
@@ -16,7 +16,7 @@
 def dims_of(cblk):
     cpad = -(-cblk // 16) * 16
     low = (cpad - cblk) // 2
-    rows = 32 if cpad % 32 == 0 and 2 * low + cblk == cpad else cpad
+    rows = 16 if cpad % 16 == 0 and 2 * low + cblk == cpad else cpad
     return cpad, low, rows
 
 
@@ -45,8 +45,8 @@
 
 
 def kernel(
-    n, cblk, x_ref, taps, filt, out,
-    xs, qmix, snd, rcv, osnd, orcv, h32, xfa, xfb, ya, yb, toep0, toep1, lhs0, lhs1, xc0, xc1,
+    n, cblk, q_hbm, k_hbm, v_hbm, taps_hbm, filt_hbm, out,
+    xin, tin, filt, in_sem, alt, taps, xf, xs, qmix, snd, rcv, osnd, orcv, h32, xfa, xfb, ya, yb, toep0, toep1, lhs0, lhs1, xc0, xc1,
     hs_sem, hr_sem, s_sem, r_sem, os_sem, or_sem,
 ):
     cpad, low, rows = dims_of(cblk)
@@ -65,14 +65,35 @@
 
     lax.fori_loop(1, n, greet, 0)
 
+    loads = [
+        pltpu.make_async_copy(src, dst, in_sem.at[i])
+        for i, (src, dst) in enumerate((
+            (q_hbm, xin.at[0]), (k_hbm, xin.at[1]), (v_hbm, xin.at[2]),
+            (taps_hbm, tin), (filt_hbm, filt),
+        ))
+    ]
+    for i in (1, 2, 3, 0, 4):
+        loads[i].start()
+
     eye = unit(False)
     flip = unit(True)
+    channels = n * cblk
+    held = 8 + channels
+    for half in range(2):
+        xc[half][:, 0:n, :] = jnp.zeros((2, n, LANES), F32)
+    taps[...] = jnp.zeros((2, 3, 8, cp), F32)
+    alt[...] = jnp.zeros((3, 8, cp), F32)
     for a in range(3):
+        xf[a, 0:8, :] = jnp.zeros((8, LANES), F32)
+        xf[a, held : held + 16, :] = jnp.zeros((16, LANES), F32)
+
+    def turn(a):
+        loads[a].wait()
+        xf[a, 8:held, :] = xin[a].astype(F32)
         for g in range(groups):
-            ls = slice(g * LANES, (g + 1) * LANES)
-            xs[a, 8 : 8 + LANES, ls] = to_time_major(eye, x_ref[a, ls, :])
-
-    pl.semaphore_wait(barrier, n - 1)
+            starts = [8 + (g * per + s) * cblk - low for s in range(per)]
+            wide = jnp.concatenate([xf[a, i : i + cpad, :] for i in starts], axis=0).astype(BF16)
+            xs[a, 8 : 8 + LANES, g * LANES : (g + 1) * LANES] = to_time_major(eye, wide)
 
     def halo(a, up):
         if up:
@@ -87,16 +108,6 @@
             device_id={"ctx": lax.rem(me + n - 1, n)},
         )
 
-    @pl.when(me < n - 1)
-    def _():
-        for a in (1, 2, 0):
-            halo(a, True).start()
-
-    @pl.when(me > 0)
-    def _():
-        for a in (1, 2, 0):
-            halo(a, False).start()
-
     @pl.when(me == 0)
     def _():
         xs[:, 0:8, :] = jnp.zeros((3, 8, cp), F32)
@@ -104,11 +115,6 @@
     @pl.when(me == n - 1)
     def _():
         xs[:, 8 + LANES : 16 + LANES, :] = jnp.zeros((3, 8, cp), F32)
-
-    for d in range(n):
-        h32[d] = filt[:, d * LANES : (d + 1) * LANES].astype(F32)
-    for half in range(2):
-        xc[half][:, 0:n, :] = jnp.zeros((2, n, LANES), F32)
 
     def halo_wait(arrays):
         @pl.when(me > 0)
@@ -120,6 +126,40 @@
         def _():
             for a in arrays:
                 halo(a, False).wait_recv()
+
+    def halo_start(arrays):
+        @pl.when(me < n - 1)
+        def _():
+            for a in arrays:
+                halo(a, True).start()
+
+        @pl.when(me > 0)
+        def _():
+            for a in arrays:
+                halo(a, False).start()
+
+    turn(1)
+    turn(2)
+    pl.semaphore_wait(barrier, n - 1)
+    halo_start((1, 2))
+    turn(0)
+    halo_start((0,))
+    loads[3].wait()
+    for ref, shift in ((taps.at[0], low), (alt, cpad - cblk - low)):
+        for b in range(n):
+            base = b * cblk - shift
+            lo, hi = max(base, 0), min(base + cpad, channels)
+            at = b * cpad + lo - base
+            ref[:, 0:TAPS, at : at + hi - lo] = tin[:, :, lo:hi]
+    turner = unit(True).astype(F32)
+    for g in range(groups):
+        source = alt[:, :, cp - (g + 1) * LANES : cp - g * LANES].reshape(24, LANES)
+        taps[1, :, :, g * LANES : (g + 1) * LANES] = jnp.dot(
+            source, turner, precision=lax.Precision.HIGHEST, preferred_element_type=F32
+        ).reshape(3, 8, LANES)
+    loads[4].wait()
+    for d in range(n):
+        h32[d] = filt[:, d * LANES : (d + 1) * LANES].astype(F32)
 
     halo_wait((1, 2))
     for g in range(groups):
@@ -257,7 +297,11 @@
             [orcv[nch - 1 - m, n - 1 - b, 1] for b in blocks for m in range(nch)], axis=0
         )
         mixed = qmix[0, :, ls] * to_time_major(eye, ma) + qmix[1, :, ls] * to_time_major(flip, mb)
-        out[ls, :] = to_channel_major(mixed.astype(BF16), eye).astype(BF16)
+        mixed = to_channel_major(mixed.astype(BF16), eye)
+        for s, b in enumerate(blocks):
+            part = mixed[s * cpad + low : s * cpad + low + cblk]
+            xf[0, 8 + b * cblk : 8 + (b + 1) * cblk, :] = part
+    out[...] = xf[0, 8:held, :].astype(BF16)
 
     for m in range(nch):
         each_peer(lambda peer: data_copy(m, peer, me).wait_send())
@@ -281,20 +325,23 @@
     cpad, low, rows = dims_of(cblk)
     nch = cpad // rows
     cp = n * cpad
-    pad = ((0, 0), (0, 0), (low, cpad - cblk - low), (0, 0))
-    x = jnp.stack([queries, key_rows, value_rows]).reshape(3, n, cblk, tokens)
-    x = jnp.pad(x, pad).reshape(3, cp, tokens)
-    taps = jnp.stack([short_taps, short_taps[:, ::-1, :]]).reshape(6, n, cblk, TAPS)
-    taps = jnp.pad(taps, pad).reshape(2, 3, cp, TAPS)
-    taps = jnp.pad(jnp.swapaxes(taps, 2, 3), ((0, 0), (0, 0), (0, 1), (0, 0)))
+    taps = jnp.swapaxes(short_taps, 1, 2)
+    hbm = pl.BlockSpec(memory_space=pltpu.MemorySpace.HBM)
     vmem = pl.BlockSpec(memory_space=pltpu.VMEM)
     dma = pltpu.SemaphoreType.DMA
-    mixed = pl.pallas_call(
+    return pl.pallas_call(
         functools.partial(kernel, n, cblk),
-        out_shape=jax.ShapeDtypeStruct((cp, tokens), BF16),
-        in_specs=[vmem] * 3,
+        out_shape=jax.ShapeDtypeStruct((channels, tokens), BF16),
+        in_specs=[hbm] * 5,
         out_specs=vmem,
         scratch_shapes=[
+            pltpu.VMEM((3, channels, tokens), BF16),
+            pltpu.VMEM((3, TAPS, channels), F32),
+            pltpu.VMEM((cblk, length), BF16),
+            dma((5,)),
+            pltpu.VMEM((3, 8, cp), F32),
+            pltpu.VMEM((2, 3, 8, cp), F32),
+            pltpu.VMEM((3, channels + 24, LANES), F32),
             pltpu.VMEM((3, LANES + 16, cp), F32),
             pltpu.VMEM((2, LANES, cp), F32),
             pltpu.VMEM((nch, n, 2, rows, LANES), BF16),
@@ -320,11 +367,9 @@
             dma((nch, n)),
         ],
         compiler_params=pltpu.CompilerParams(
-            collective_id=0, has_side_effects=True, vmem_limit_bytes=48 * 1024 * 1024
+            collective_id=0, has_side_effects=True, vmem_limit_bytes=62 * 1024 * 1024
         ),
-    )(x, taps, long_filter)
-    mixed = mixed.reshape(n, cpad, tokens)[:, low : low + cblk]
-    return mixed.reshape(channels, tokens)
+    )(queries, key_rows, value_rows, taps, long_filter)
 
 
 def solution(mesh):

time: 50.3 us -> 46.5 us (0.924)
  local copies, waits for them, and re-layouts: 5.33 us -> 1.65 us
    another operation x4 -> x0, local copies, waits for them, and re-layouts: 2.16 us -> none  [the longest x3 2.07 us: on_device(): x = jnp.stack([queries, key_rows, value_rows]).reshape(3, n, cblk, tokens)]
    reshape x3 -> x0, local copies, waits for them, and re-layouts: 1.17 us -> none  [the longest x1 0.74 us: on_device(): return mixed.reshape(channels, tokens)]
    unnamed x7 -> x1, local copies, waits for them, and re-layouts: 1.76 us -> 1.65 us
where the time goes in v3:
time: 46.5 us; the launch traced here: 46.3 us
  Pallas kernels  44.6 us (96%)
  local copies, waits for them, and re-layouts  1.65 us (4%)
    pallas_call x1, Pallas kernels, on_device(): pl.pallas_call(functools.partial(kernel, n, cblk), out_shape=jax.ShapeDty...  44.6 us
    unnamed x1, local copies, waits for them, and re-layouts  1.65 us

profile of v3, /device:TPU:0, one launch (start us, length us, event | category | flops | bytes accessed | tf_op | source)
XLA Modules:
  0.0 46.3 jit_solution(271072828329864260)
XLA Ops:
  0.0 44.6 %shard_map.55 = bf16[960,128]{1,0:T(8,128)(2,1)} custom-call(bf16[960,128]{1,0:T(8,128)(2,1)} %q_hbm.1, bf16[960,128]{1,0:T(8,128)(2,1)} %k_hbm.1, bf16[960,128]{1,0:T(8,128)(2,1)} %v_hbm.1, f32[3,7,960]{2,1,0:T(8,128)} %bitcast.1, bf16[60,2048]{1,0:T(8,128)(2,1)} %filt_hbm.1), custom_call_target="tpu_custom_call" | custom-call | tf_op jit(solution)/shard_map/pallas_call | solution.py:332
  44.7 1.7 %copy.7 = bf16[960,128]{1,0:T(8,128)(2,1)} copy(bf16[960,128]{1,0:T(8,128)(2,1)} %shard_map.55) | data formatting | bytes 491520

commit v4 on v3

--- a/solution.py
+++ b/solution.py
@@ -178,16 +178,29 @@
     def data_copy(m, dest, slot):
         return pltpu.make_async_remote_copy(
             src_ref=snd.at[m, dest], dst_ref=rcv.at[m, slot],
-            send_sem=s_sem.at[m, dest], recv_sem=r_sem.at[m, slot],
+            send_sem=s_sem.at[m], recv_sem=r_sem.at[m],
             device_id={"ctx": dest},
         )
 
     def back_copy(m, dest, slot):
         return pltpu.make_async_remote_copy(
             src_ref=osnd.at[m, dest], dst_ref=orcv.at[m, slot],
-            send_sem=os_sem.at[m, dest], recv_sem=or_sem.at[m, slot],
+            send_sem=os_sem.at[m], recv_sem=or_sem.at[m],
             device_id={"ctx": dest},
         )
+
+    def all_of(m, src, dst, send_sem, recv_sem):
+        return pltpu.make_async_remote_copy(
+            src_ref=src.at[m, pl.ds(0, n - 1)], dst_ref=dst.at[m, pl.ds(0, n - 1)],
+            send_sem=send_sem.at[m], recv_sem=recv_sem.at[m],
+            device_id={"ctx": lax.rem(me + 1, n)},
+        )
+
+    def all_data(m):
+        return all_of(m, snd, rcv, s_sem, r_sem)
+
+    def all_back(m):
+        return all_of(m, osnd, orcv, os_sem, or_sem)
 
     def each_peer(act):
         def step(o, carry):
@@ -210,7 +223,7 @@
     causal = col_id >= row_id
 
     for m in range(nch):
-        each_peer(lambda peer: data_copy(m, me, peer).wait_recv())
+        all_data(m).wait_recv()
         rcv[m, me] = snd[m, me]
 
         def widen(src, carry):
@@ -287,7 +300,7 @@
         orcv[m, me] = osnd[m, me]
 
     for m in range(nch):
-        each_peer(lambda peer: back_copy(m, me, peer).wait_recv())
+        all_back(m).wait_recv()
 
     for g in range(groups):
         ls = slice(g * LANES, (g + 1) * LANES)
@@ -304,8 +317,8 @@
     out[...] = xf[0, 8:held, :].astype(BF16)
 
     for m in range(nch):
-        each_peer(lambda peer: data_copy(m, peer, me).wait_send())
-        each_peer(lambda peer: back_copy(m, peer, me).wait_send())
+        all_data(m).wait_send()
+        all_back(m).wait_send()
 
     @pl.when(me < n - 1)
     def _():
@@ -361,10 +374,10 @@
             pltpu.VMEM((2, 2 * n, LANES), F32),
             dma((2, 3)),
             dma((2, 3)),
-            dma((nch, n)),
-            dma((nch, n)),
-            dma((nch, n)),
-            dma((nch, n)),
+            dma((nch,)),
+            dma((nch,)),
+            dma((nch,)),
+            dma((nch,)),
         ],
         compiler_params=pltpu.CompilerParams(
             collective_id=0, has_side_effects=True, vmem_limit_bytes=62 * 1024 * 1024

time: 46.5 us -> 42.8 us (0.920)
  Pallas kernels: 44.6 us -> 41 us
    pallas_call x1, Pallas kernels: 44.6 us -> 41 us  [on_device(): pl.pallas_call(functools.partial(kernel, n, cblk), out_shape=jax.ShapeDty...]
where the time goes in v4:
time: 42.8 us; the launch traced here: 42.6 us
  Pallas kernels  41 us (96%)
  local copies, waits for them, and re-layouts  1.65 us (4%)
    pallas_call x1, Pallas kernels, on_device(): pl.pallas_call(functools.partial(kernel, n, cblk), out_shape=jax.ShapeDty...  41 us
    unnamed x1, local copies, waits for them, and re-layouts  1.65 us

profile of v4, /device:TPU:0, one launch (start us, length us, event | category | flops | bytes accessed | tf_op | source)
XLA Modules:
  0.0 42.6 jit_solution(15873709673213982987)
XLA Ops:
  0.0 41.0 %shard_map.55 = bf16[960,128]{1,0:T(8,128)(2,1)} custom-call(bf16[960,128]{1,0:T(8,128)(2,1)} %q_hbm.1, bf16[960,128]{1,0:T(8,128)(2,1)} %k_hbm.1, bf16[960,128]{1,0:T(8,128)(2,1)} %v_hbm.1, f32[3,7,960]{2,1,0:T(8,128)} %bitcast.1, bf16[60,2048]{1,0:T(8,128)(2,1)} %filt_hbm.1), custom_call_target="tpu_custom_call" | custom-call | tf_op jit(solution)/shard_map/pallas_call | solution.py:345
  41.0 1.7 %copy.7 = bf16[960,128]{1,0:T(8,128)(2,1)} copy(bf16[960,128]{1,0:T(8,128)(2,1)} %shard_map.55) | data formatting | bytes 491520

commit v5 on v4

--- a/solution.py
+++ b/solution.py
@@ -207,7 +207,7 @@
             act(lax.rem(me + o, n))
             return carry
 
-        lax.fori_loop(1, n, step, 0)
+        lax.fori_loop(1, n, step, 0, unroll=3)
 
     for m in range(nch):
         each_peer(lambda peer: data_copy(m, peer, me).start())
@@ -233,7 +233,7 @@
             xfb[pl.ds(at, rows), :] = rcv[m, src, 1].astype(F32)
             return carry
 
-        lax.fori_loop(0, n, widen, 0, unroll=4)
+        lax.fori_loop(0, n, widen, 0, unroll=8)
 
         first = max(m * rows, low)
         last = min((m + 1) * rows, low + cblk)
@@ -295,7 +295,7 @@
             osnd[m, dest, 1] = yb[pl.ds(at, rows), :].astype(BF16)
             return carry
 
-        lax.fori_loop(0, n, narrow, 0, unroll=4)
+        lax.fori_loop(0, n, narrow, 0, unroll=8)
         each_peer(lambda peer: back_copy(m, peer, me).start())
         orcv[m, me] = osnd[m, me]
 

time: 42.8 us -> 42.6 us (level)
  no operation moved by 1% of the time
where the time goes in v5:
time: 42.6 us; the launch traced here: 42.4 us
  Pallas kernels  40.8 us (96%)
  local copies, waits for them, and re-layouts  1.65 us (4%)
    pallas_call x1, Pallas kernels, on_device(): pl.pallas_call(functools.partial(kernel, n, cblk), out_shape=jax.ShapeDty...  40.8 us
    unnamed x1, local copies, waits for them, and re-layouts  1.65 us

profile of v5, /device:TPU:0, one launch (start us, length us, event | category | flops | bytes accessed | tf_op | source)
XLA Modules:
  0.0 42.4 jit_solution(2741760931621459311)
XLA Ops:
  0.0 40.8 %shard_map.55 = bf16[960,128]{1,0:T(8,128)(2,1)} custom-call(bf16[960,128]{1,0:T(8,128)(2,1)} %q_hbm.1, bf16[960,128]{1,0:T(8,128)(2,1)} %k_hbm.1, bf16[960,128]{1,0:T(8,128)(2,1)} %v_hbm.1, f32[3,7,960]{2,1,0:T(8,128)} %bitcast.1, bf16[60,2048]{1,0:T(8,128)(2,1)} %filt_hbm.1), custom_call_target="tpu_custom_call" | custom-call | tf_op jit(solution)/shard_map/pallas_call | solution.py:345
  40.8 1.7 %copy.7 = bf16[960,128]{1,0:T(8,128)(2,1)} copy(bf16[960,128]{1,0:T(8,128)(2,1)} %shard_map.55) | data formatting | bytes 491520
